TPU v7x, 32 devices: a whole 2x2x4 slice. The times are simulated.
32 devices in a mesh: dev: 32 (over z, y, x, core).
Axes of the slice: x: 2, y: 2, z: 4, core: 2. Of those that a mesh axis runs over, the one named last changes fastest.
Arguments:
- images: bfloat16 [256, 768, 1536], P('dev'), may hold values from -6 to 6
- legendre: bfloat16 [32, 704, 768], P('dev'), may hold values from -0.21875 to 0.21875
- leakage: float32 [32, 3, 13, 704], P('dev'), may hold values from -1 to 1
Outputs:
- modes: float32 [32, 704, 512], P('dev')
All inputs are finite; a program needn't handle non-finite values.
Results may differ from a plain program's by a relative error of at most 0.0053.
Values may be sent and summed in bfloat16 or wider, within the bound.
A program may use at most 128 MiB of HBM per device.

v0:
```python
import math
import jax
import jax.numpy as jnp
from jax import lax
from jax.sharding import PartitionSpec as P

BLK = 64
BAND = 6


def padded_2(cells, sides, width):
    for axis, dim in sides:
        count = lax.axis_size(axis)
        ends = count - 1
        head = lax.slice_in_dim(cells, 0, width, axis=dim)
        tail = lax.slice_in_dim(cells, cells.shape[dim] - width, cells.shape[dim], axis=dim)
        cells = jnp.concatenate(
            [
                lax.ppermute(tail, axis, [(i, (i + 1) % count) for i in range(ends)]),
                cells,
                lax.ppermute(head, axis, [((i + 1) % count, i) for i in range(ends)]),
            ],
            axis=dim,
        )
    return cells


def lon_table(nlon, norders):
    index = jnp.arange(nlon, dtype=jnp.int32)[None, :]
    order = jnp.arange(norders, dtype=jnp.int32)[:, None]
    phase = (index * order % nlon).astype(jnp.float32)
    angle = 2.0 * math.pi * phase / nlon
    table = jnp.stack([jnp.cos(angle), -jnp.sin(angle)], axis=1) / math.sqrt(nlon)
    return table.reshape(2 * norders, nlon).astype(jnp.bfloat16)


def time_table(ntimes):
    index = jnp.arange(ntimes, dtype=jnp.int32)
    phase = (index[:, None] * index[None, :] % ntimes).astype(jnp.float32)
    angle = 2.0 * math.pi * phase / ntimes
    cosine = jnp.cos(angle)
    sine = jnp.sin(angle)
    upper = jnp.concatenate([cosine, -sine], axis=1)
    lower = jnp.concatenate([sine, cosine], axis=1)
    return (jnp.concatenate([upper, lower], axis=0) / math.sqrt(ntimes)).astype(jnp.bfloat16)


def transform_images(table, block):
    out = jnp.einsum("kn,tan->kta", table, block, preferred_element_type=jnp.float32)
    return out.astype(jnp.bfloat16)


def on_device(images, legendre, leakage):
    devices = lax.axis_size("dev")
    here = lax.axis_index("dev")
    t_local, nlat, nlon = images.shape
    m_local, degrees_all, _ = legendre.shape
    norders = m_local * devices
    ntimes = t_local * devices
    table = lon_table(nlon, norders)
    whole = transform_images(table, images).reshape(norders, 2, t_local, nlat)
    gathered = lax.all_to_all(whole, "dev", split_axis=0, concat_axis=2, tiled=True)
    wtable = time_table(ntimes)
    nblocks = degrees_all // BLK
    local = 0
    order = here * m_local + local
    flat = gathered[local].reshape(2 * ntimes, nlat)
    rows_table = legendre[local]

    def one_block(block, spectra, order=order, flat=flat, rows_table=rows_table):
        start = block * BLK
        rows = lax.dynamic_slice_in_dim(rows_table, start, BLK, 0)
        coef = lax.dot_general(
            rows, flat, (((1,), (1,)), ((), ())), preferred_element_type=jnp.float32
        )
        degree = start + jnp.arange(BLK, dtype=jnp.int32)
        coef = jnp.where((degree >= order)[:, None], coef, jnp.float32(0.0)).astype(jnp.bfloat16)
        result = jnp.dot(coef, wtable, preferred_element_type=jnp.float32)
        return lax.dynamic_update_slice_in_dim(spectra, result, start, 0)

    first = order // BLK
    empty = jnp.zeros((degrees_all, 2 * ntimes), jnp.float32)
    spectra_list = [lax.fori_loop(first, jnp.int32(nblocks), one_block, empty)]
    spectra = jnp.stack(spectra_list, axis=0)
    padded = padded_2(spectra, (("dev", 0),), 1)
    padded = jnp.pad(padded, ((0, 0), (BAND, BAND), (0, 0)))
    degrees = jnp.arange(degrees_all, dtype=jnp.int32)
    local = 0
    order = here * m_local + local
    coeffs = leakage[local]
    total = jnp.zeros((degrees_all, 2 * ntimes), jnp.float32)
    for shift in range(3):
        for offset in range(2 * BAND + 1):
            total = (
                total
                + coeffs[shift, offset][:, None]
                * padded[local + shift, offset : offset + degrees_all]
            )
    outputs = [jnp.where((degrees >= order)[:, None], total, jnp.float32(0.0))]
    return jnp.stack(outputs, axis=0)


def solution(mesh):
    placed = (P("dev", None, None), P("dev", None, None), P("dev", None, None, None))
    return jax.shard_map(
        on_device, mesh=mesh, in_specs=placed, out_specs=P("dev", None, None), check_vma=False
    )
```

profile of v0, /device:TPU:1, one launch (start us, length us, event | category | flops | bytes accessed | tf_op | source)
XLA Modules:
  0.0 104.0 jit_solution(8679333870553698052)
XLA Ops:
  0.0 0.8 sine_negate_fusion
  0.9 0.2 copy.10
  1.1 0.1 reshape.393
  1.2 12.1 %convolution_convert_fusion = bf16[64,8,768]{2,0,1:T(8,128)(2,1)S(1)} fusion(bf16[64,1536,1]{1,0,2:T(8,128)(2,1)S(1)} %reshape.393, bf16[8,768,1536]{2,1,0:T(8,128)(2,1)} %param.5), kind=kOutput, calls=%fused_computation.89 | convolution fusion | flops 1208352768 | bytes 19857408 | tf_op jit(solution)/shard_map/kn,tan->kta/dot_general | solution.py:49
  13.3 0.3 reshape.392
  13.6 1.4 %copy.11 = bf16[32,2,8,768]{3,1,2,0:T(2,128)(2,1)} copy(bf16[32,2,8,768]{3,1,0,2:T(2,128)(2,1)S(1)} %reshape.392) | data formatting | bytes 1572864 | tf_op jit(solution)/shard_map/reshape | solution.py:61
  15.0 7.1 %all-to-all-start = ((bf16[32,2,8,768]{3,1,2,0:T(2,128)(2,1)}), bf16[32,2,8,768]{3,1,2,0:T(2,128)(2,1)S(1)}, u32[]{:S(2)}, u32[]{:S(2)}) async-start(bf16[32,2,8,768]{3,1,2,0:T(2,128)(2,1)} %copy.11), calls=%async_computation | async-start | bytes 1572864 | tf_op jit(solution)/shard_map/all_to_all | solution.py:62
  22.1 1.0 fusion.64
  23.1 1.0 fusion.62
  24.2 18.1 %all-to-all-done = bf16[32,2,8,768]{3,1,2,0:T(2,128)(2,1)S(1)} async-done(((bf16[32,2,8,768]{3,1,2,0:T(2,128)(2,1)}), bf16[32,2,8,768]{3,1,2,0:T(2,128)(2,1)S(1)}, u32[]{:S(2)}, u32[]{:S(2)}) %all-to-all-start) | async-done | bytes 786464 | tf_op jit(solution)/shard_map/all_to_all | solution.py:62
  42.3 0.1 copy.12
  42.4 0.2 broadcast_in_dim.34
  42.6 16.0 %while.10 = (s32[]{:T(128)}, f32[704,512]{1,0:T(8,128)S(1)}, s32[]{:T(128)}, bf16[704,768]{1,0:T(8,128)(2,1)}, bf16[512,768]{1,0:T(8,128)(2,1)S(1)}, /*index=5*/...) while((s32[]{:T(128)}, f32[704,512]{1,0:T(8,128)S(1)}, s32[]{:T(128)}, ...), condition=%wide.region_1.2_spmd, body=%wide.region_0.1_spmd.sunk | while | flops 83951752 | bytes 1541851 | solution.py:83
  42.6 1.4 %convolution_dynamic-update-slice_fusion.2 = f32[704,512]{1,0:T(8,128)S(1)} fusion(f32[704,512]{1,0:T(8,128)S(1)} %get-tuple-element.140, s32[]{:T(128)S(6)} %select_n.82, bf16[512,512]{1,0:T(8,128)(2,1)S(1)} %get-tuple-element.154, bf16[512,768]{1,0:T(8,128)(2,1)S(1)} %get-tuple-element.153, bf16[704,768]{1,0:T(8,128)(2,1)} %get-tuple-element.152, ...), kind=kOutput, calls=%fused_computation.clone.1 | convolution fusion | flops 83951616 | bytes 1541632 | tf_op jit(solution)/shard_map/while/body/dot_general | solution.py:78
  44.1 1.4 %convolution_dynamic-update-slice_fusion.2 = f32[704,512]{1,0:T(8,128)S(1)} fusion(f32[704,512]{1,0:T(8,128)S(1)} %get-tuple-element.140, s32[]{:T(128)S(6)} %select_n.82, bf16[512,512]{1,0:T(8,128)(2,1)S(1)} %get-tuple-element.154, bf16[512,768]{1,0:T(8,128)(2,1)S(1)} %get-tuple-element.153, bf16[704,768]{1,0:T(8,128)(2,1)} %get-tuple-element.152, ...), kind=kOutput, calls=%fused_computation.clone.1 | convolution fusion | flops 83951616 | bytes 1541632 | tf_op jit(solution)/shard_map/while/body/dot_general | solution.py:78
  45.5 1.4 %convolution_dynamic-update-slice_fusion.2 = f32[704,512]{1,0:T(8,128)S(1)} fusion(f32[704,512]{1,0:T(8,128)S(1)} %get-tuple-element.140, s32[]{:T(128)S(6)} %select_n.82, bf16[512,512]{1,0:T(8,128)(2,1)S(1)} %get-tuple-element.154, bf16[512,768]{1,0:T(8,128)(2,1)S(1)} %get-tuple-element.153, bf16[704,768]{1,0:T(8,128)(2,1)} %get-tuple-element.152, ...), kind=kOutput, calls=%fused_computation.clone.1 | convolution fusion | flops 83951616 | bytes 1541632 | tf_op jit(solution)/shard_map/while/body/dot_general | solution.py:78
  47.0 1.4 %convolution_dynamic-update-slice_fusion.2 = f32[704,512]{1,0:T(8,128)S(1)} fusion(f32[704,512]{1,0:T(8,128)S(1)} %get-tuple-element.140, s32[]{:T(128)S(6)} %select_n.82, bf16[512,512]{1,0:T(8,128)(2,1)S(1)} %get-tuple-element.154, bf16[512,768]{1,0:T(8,128)(2,1)S(1)} %get-tuple-element.153, bf16[704,768]{1,0:T(8,128)(2,1)} %get-tuple-element.152, ...), kind=kOutput, calls=%fused_computation.clone.1 | convolution fusion | flops 83951616 | bytes 1541632 | tf_op jit(solution)/shard_map/while/body/dot_general | solution.py:78
  48.4 1.4 %convolution_dynamic-update-slice_fusion.2 = f32[704,512]{1,0:T(8,128)S(1)} fusion(f32[704,512]{1,0:T(8,128)S(1)} %get-tuple-element.140, s32[]{:T(128)S(6)} %select_n.82, bf16[512,512]{1,0:T(8,128)(2,1)S(1)} %get-tuple-element.154, bf16[512,768]{1,0:T(8,128)(2,1)S(1)} %get-tuple-element.153, bf16[704,768]{1,0:T(8,128)(2,1)} %get-tuple-element.152, ...), kind=kOutput, calls=%fused_computation.clone.1 | convolution fusion | flops 83951616 | bytes 1541632 | tf_op jit(solution)/shard_map/while/body/dot_general | solution.py:78
  49.9 1.4 %convolution_dynamic-update-slice_fusion.2 = f32[704,512]{1,0:T(8,128)S(1)} fusion(f32[704,512]{1,0:T(8,128)S(1)} %get-tuple-element.140, s32[]{:T(128)S(6)} %select_n.82, bf16[512,512]{1,0:T(8,128)(2,1)S(1)} %get-tuple-element.154, bf16[512,768]{1,0:T(8,128)(2,1)S(1)} %get-tuple-element.153, bf16[704,768]{1,0:T(8,128)(2,1)} %get-tuple-element.152, ...), kind=kOutput, calls=%fused_computation.clone.1 | convolution fusion | flops 83951616 | bytes 1541632 | tf_op jit(solution)/shard_map/while/body/dot_general | solution.py:78
  51.3 1.4 %convolution_dynamic-update-slice_fusion.2 = f32[704,512]{1,0:T(8,128)S(1)} fusion(f32[704,512]{1,0:T(8,128)S(1)} %get-tuple-element.140, s32[]{:T(128)S(6)} %select_n.82, bf16[512,512]{1,0:T(8,128)(2,1)S(1)} %get-tuple-element.154, bf16[512,768]{1,0:T(8,128)(2,1)S(1)} %get-tuple-element.153, bf16[704,768]{1,0:T(8,128)(2,1)} %get-tuple-element.152, ...), kind=kOutput, calls=%fused_computation.clone.1 | convolution fusion | flops 83951616 | bytes 1541632 | tf_op jit(solution)/shard_map/while/body/dot_general | solution.py:78
  52.8 1.4 %convolution_dynamic-update-slice_fusion.2 = f32[704,512]{1,0:T(8,128)S(1)} fusion(f32[704,512]{1,0:T(8,128)S(1)} %get-tuple-element.140, s32[]{:T(128)S(6)} %select_n.82, bf16[512,512]{1,0:T(8,128)(2,1)S(1)} %get-tuple-element.154, bf16[512,768]{1,0:T(8,128)(2,1)S(1)} %get-tuple-element.153, bf16[704,768]{1,0:T(8,128)(2,1)} %get-tuple-element.152, ...), kind=kOutput, calls=%fused_computation.clone.1 | convolution fusion | flops 83951616 | bytes 1541632 | tf_op jit(solution)/shard_map/while/body/dot_general | solution.py:78
  54.2 1.4 %convolution_dynamic-update-slice_fusion.2 = f32[704,512]{1,0:T(8,128)S(1)} fusion(f32[704,512]{1,0:T(8,128)S(1)} %get-tuple-element.140, s32[]{:T(128)S(6)} %select_n.82, bf16[512,512]{1,0:T(8,128)(2,1)S(1)} %get-tuple-element.154, bf16[512,768]{1,0:T(8,128)(2,1)S(1)} %get-tuple-element.153, bf16[704,768]{1,0:T(8,128)(2,1)} %get-tuple-element.152, ...), kind=kOutput, calls=%fused_computation.clone.1 | convolution fusion | flops 83951616 | bytes 1541632 | tf_op jit(solution)/shard_map/while/body/dot_general | solution.py:78
  55.7 1.4 %convolution_dynamic-update-slice_fusion.2 = f32[704,512]{1,0:T(8,128)S(1)} fusion(f32[704,512]{1,0:T(8,128)S(1)} %get-tuple-element.140, s32[]{:T(128)S(6)} %select_n.82, bf16[512,512]{1,0:T(8,128)(2,1)S(1)} %get-tuple-element.154, bf16[512,768]{1,0:T(8,128)(2,1)S(1)} %get-tuple-element.153, bf16[704,768]{1,0:T(8,128)(2,1)} %get-tuple-element.152, ...), kind=kOutput, calls=%fused_computation.clone.1 | convolution fusion | flops 83951616 | bytes 1541632 | tf_op jit(solution)/shard_map/while/body/dot_general | solution.py:78
  57.1 1.4 %convolution_dynamic-update-slice_fusion.2 = f32[704,512]{1,0:T(8,128)S(1)} fusion(f32[704,512]{1,0:T(8,128)S(1)} %get-tuple-element.140, s32[]{:T(128)S(6)} %select_n.82, bf16[512,512]{1,0:T(8,128)(2,1)S(1)} %get-tuple-element.154, bf16[512,768]{1,0:T(8,128)(2,1)S(1)} %get-tuple-element.153, bf16[704,768]{1,0:T(8,128)(2,1)} %get-tuple-element.152, ...), kind=kOutput, calls=%fused_computation.clone.1 | convolution fusion | flops 83951616 | bytes 1541632 | tf_op jit(solution)/shard_map/while/body/dot_general | solution.py:78
  58.6 2.5 %collective-permute-start.1 = (f32[1,704,512]{2,1,0:T(8,128)S(1)}, f32[1,704,512]{2,1,0:T(8,128)S(1)}, u32[]{:S(2)}, u32[]{:S(2)}) collective-permute-start(f32[1,704,512]{2,1,0:T(8,128)S(1)} %bitcast.23), channel_id=1, source_target_pairs={{1,0},{2,1},{3,2},{4,3},{5,4},{6,5},{7,6},{8,7},{9,8},{10,9},{11,1... | collective-permute-start | bytes 4325384 | tf_op jit(solution)/shard_map/ppermute | solution.py:21
  61.1 3.0 %collective-permute-start = (f32[1,704,512]{2,1,0:T(8,128)S(1)}, f32[1,704,512]{2,1,0:T(8,128)S(1)}, u32[]{:S(2)}, u32[]{:S(2)}) collective-permute-start(f32[1,704,512]{2,1,0:T(8,128)S(1)} %bitcast.24), channel_id=1, source_target_pairs={{0,1},{1,2},{2,3},{3,4},{4,5},{5,6},{6,7},{7,8},{8,9},{9,10},{10,1... | collective-permute-start | bytes 4325384 | tf_op jit(solution)/shard_map/ppermute | solution.py:19
  64.2 0.2 slice_reduce_fusion.38
  64.4 0.2 slice_reduce_fusion.37
  64.5 25.7 %collective-permute-done.1 = f32[1,704,512]{2,1,0:T(8,128)S(1)} collective-permute-done((f32[1,704,512]{2,1,0:T(8,128)S(1)}, f32[1,704,512]{2,1,0:T(8,128)S(1)}, u32[]{:S(2)}, u32[]{:S(2)}) %collective-permute-start.1) | collective-permute-done | bytes 1441824 | tf_op jit(solution)/shard_map/ppermute | solution.py:21
  90.3 4.8 %collective-permute-done = f32[1,704,512]{2,1,0:T(8,128)S(1)} collective-permute-done((f32[1,704,512]{2,1,0:T(8,128)S(1)}, f32[1,704,512]{2,1,0:T(8,128)S(1)}, u32[]{:S(2)}, u32[]{:S(2)}) %collective-permute-start) | collective-permute-done | bytes 1441824 | tf_op jit(solution)/shard_map/ppermute | solution.py:19
  95.1 0.6 select_maximum_fusion
  95.7 8.4 %fusion.10 = f32[1,704,512]{2,1,0:T(8,128)} fusion(f32[3,716,512]{2,1,0:T(8,128)S(1)} %select_maximum_fusion, f32[1,704,512]{2,1,0:T(8,128)S(1)} %collective-permute-done.1, f32[704,512]{1,0:T(8,128)S(1)} %get-tuple-element.37, f32[1,704,512]{2,1,0:T(8,128)S(1)} %collective-permute-done, f32[704]{0:T(1024)S(1)} %get-tuple-element.39, ...), kind=kLoop, calls=%fused_computation.16 | loop fusion | flops 28114944 | bytes 57782208 | tf_op jit(solution)/shard_map/jit(_where)/select_n | solution.py:99
  (18 shorter events, 0.2 us)
Async XLA Ops:
  15.0 27.3 %all-to-all-start = ((bf16[32,2,8,768]{3,1,2,0:T(2,128)(2,1)}), bf16[32,2,8,768]{3,1,2,0:T(2,128)(2,1)S(1)}, u32[]{:S(2)}, u32[]{:S(2)}) async-start(bf16[32,2,8,768]{3,1,2,0:T(2,128)(2,1)} %copy.11), calls=%async_computation | async-start | bytes 1572864 | tf_op jit(solution)/shard_map/all_to_all | solution.py:62
  42.6 21.6 %copy-start = (f32[1,3,13,704]{3,0,2,1:T(1,128)S(1)}, f32[1,3,13,704]{3,0,2,1:T(1,128)}, u32[]{:S(2)}) copy-start(f32[1,3,13,704]{3,0,2,1:T(1,128)} %param.7) | copy-start | bytes 329476
  58.6 31.7 %collective-permute-start.1 = (f32[1,704,512]{2,1,0:T(8,128)S(1)}, f32[1,704,512]{2,1,0:T(8,128)S(1)}, u32[]{:S(2)}, u32[]{:S(2)}) collective-permute-start(f32[1,704,512]{2,1,0:T(8,128)S(1)} %bitcast.23), channel_id=1, source_target_pairs={{1,0},{2,1},{3,2},{4,3},{5,4},{6,5},{7,6},{8,7},{9,8},{10,9},{11,1... | collective-permute-start | bytes 4325384 | tf_op jit(solution)/shard_map/ppermute | solution.py:21
  61.1 34.0 %collective-permute-start = (f32[1,704,512]{2,1,0:T(8,128)S(1)}, f32[1,704,512]{2,1,0:T(8,128)S(1)}, u32[]{:S(2)}, u32[]{:S(2)}) collective-permute-start(f32[1,704,512]{2,1,0:T(8,128)S(1)} %bitcast.24), channel_id=1, source_target_pairs={{0,1},{1,2},{2,3},{3,4},{4,5},{5,6},{6,7},{7,8},{8,9},{9,10},{10,1... | collective-permute-start | bytes 4325384 | tf_op jit(solution)/shard_map/ppermute | solution.py:19
where the time goes:
time: 105 us; the launch traced here: 104 us
  waiting for transfers between devices  48.7 us (46%)
  matrix products  27.6 us (26%)
  starting transfers between devices  12.6 us (12%)
  other arithmetic  11.9 us (11%)
  local copies, waits for them, and re-layouts  2.61 us (2%)
    ppermute x1, waiting for transfers between devices, padded_2(): lax.ppermute(head, axis, [((i + 1) % count, i) for i in range(ends)])  25.7 us
    all_to_all x1, waiting for transfers between devices, on_device(): lax.all_to_all(whole, 'dev', split_axis=0, concat_axis=2, tiled=True)  18.1 us
    dot_general x11, matrix products, one_block(): result = jnp.dot(coef, wtable, preferred_element_type=jnp.float32)  15.5 us
    dot_general x1, matrix products, transform_images(): jnp.einsum('kn,tan->kta', table, block, preferred_element_type=jnp.float32)  12.1 us
    select_n x1, other arithmetic, on_device(): outputs = [jnp.where((degrees >= order)[:, None], total, jnp.float32(0.0))]  8.38 us
    all_to_all x1, starting transfers between devices, on_device(): lax.all_to_all(whole, 'dev', split_axis=0, concat_axis=2, tiled=True)  7.08 us
    ppermute x1, waiting for transfers between devices, padded_2(): lax.ppermute(tail, axis, [(i, (i + 1) % count) for i in range(ends)])  4.81 us
    ppermute x1, starting transfers between devices, padded_2(): lax.ppermute(tail, axis, [(i, (i + 1) % count) for i in range(ends)])  3.03 us
  transfers between devices with their start and end apart: 3, of which 3 were waited for; matrix products, arithmetic and copies ran while one was open for 2% of the time, Pallas kernels for 0%

commit v1 on v0

--- a/solution.py
+++ b/solution.py
@@ -59,7 +59,10 @@
     ntimes = t_local * devices
     table = lon_table(nlon, norders)
     whole = transform_images(table, images).reshape(norders, 2, t_local, nlat)
-    gathered = lax.all_to_all(whole, "dev", split_axis=0, concat_axis=2, tiled=True)
+    gathered = jnp.concatenate(
+        lax.all_to_all(jnp.stack(jnp.split(whole, lax.axis_size("dev"), axis=0)), "dev", 0, 0),
+        axis=2,
+    )
     wtable = time_table(ntimes)
     nblocks = degrees_all // BLK
     local = 0

time: 105 us -> 123 us (1.17)
  local copies, waits for them, and re-layouts: 2.61 us -> 21.1 us
    unnamed x3 -> x34, local copies, waits for them, and re-layouts: 0.02 us -> 19.6 us
    reshape x2 -> x1, local copies, waits for them, and re-layouts: 1.72 us -> 0.08 us  [on_device(): jnp.concatenate(lax.all_to_all(jnp.stack(jnp.split(whole, lax.axis_size('...]
where the time goes in v1:
time: 123 us
  waiting for transfers between devices  48.7 us (40%)
  matrix products  27.6 us (22%)
  local copies, waits for them, and re-layouts  21.1 us (17%)
  starting transfers between devices  12.6 us (10%)
  other arithmetic  11.9 us (10%)
    ppermute x1, waiting for transfers between devices, padded_2(): lax.ppermute(head, axis, [((i + 1) % count, i) for i in range(ends)])  25.7 us
    unnamed x34, local copies, waits for them, and re-layouts  19.6 us
    all_to_all x1, waiting for transfers between devices, on_device(): lax.all_to_all(jnp.stack(jnp.split(whole, lax.axis_size('dev'), axis=0)),...  18.1 us
    dot_general x11, matrix products, one_block(): result = jnp.dot(coef, wtable, preferred_element_type=jnp.float32)  15.5 us
    dot_general x1, matrix products, transform_images(): jnp.einsum('kn,tan->kta', table, block, preferred_element_type=jnp.float32)  12.1 us
    select_n x1, other arithmetic, on_device(): outputs = [jnp.where((degrees >= order)[:, None], total, jnp.float32(0.0))]  8.38 us
    all_to_all x1, starting transfers between devices, on_device(): lax.all_to_all(jnp.stack(jnp.split(whole, lax.axis_size('dev'), axis=0)),...  7.08 us
    ppermute x1, waiting for transfers between devices, padded_2(): lax.ppermute(tail, axis, [(i, (i + 1) % count) for i in range(ends)])  4.81 us
  transfers between devices with their start and end apart: 3, of which 3 were waited for; matrix products, arithmetic and copies ran while one was open for 2% of the time, Pallas kernels for 0%

profile of v1, /device:TPU:1, one launch (start us, length us, event | category | flops | bytes accessed | tf_op | source)
XLA Modules:
  0.0 122.6 jit_solution(4218115279579190836)
XLA Ops:
  0.0 0.8 sine_negate_fusion
  1.2 12.1 %convolution_convert_fusion = bf16[64,8,768]{2,0,1:T(8,128)(2,1)S(1)} fusion(bf16[64,1536,1]{1,0,2:T(8,128)(2,1)S(1)} %reshape.457, bf16[8,768,1536]{2,1,0:T(8,128)(2,1)} %param.5), kind=kOutput, calls=%fused_computation.89 | convolution fusion | flops 1208352768 | bytes 19857408 | tf_op jit(solution)/shard_map/kn,tan->kta/dot_general | solution.py:49
  13.9 0.6 constant_dynamic-update-slice_fusion.30
  16.4 0.6 constant_dynamic-update-slice_fusion.26
  17.1 0.6 constant_dynamic-update-slice_fusion.25
  17.7 0.6 constant_dynamic-update-slice_fusion.24
  20.2 0.6 constant_dynamic-update-slice_fusion.20
  21.5 0.6 constant_dynamic-update-slice_fusion.18
  22.1 0.6 constant_dynamic-update-slice_fusion.17
  22.8 0.6 constant_dynamic-update-slice_fusion.16
  25.3 0.6 constant_dynamic-update-slice_fusion.12
  33.6 7.1 %all-to-all-start = ((bf16[32,1,2,8,768]{4,2,3,1,0:T(2,128)(2,1)}), bf16[32,1,2,8,768]{4,2,3,1,0:T(2,128)(2,1)S(1)}, u32[]{:S(2)}, u32[]{:S(2)}) async-start(bf16[32,1,2,8,768]{4,2,3,1,0:T(2,128)(2,1)} %constant_dynamic-update-slice_fusion), calls=%async_computation | async-start | bytes 1572864 | tf_op jit(solution)/shard_map/all_to_all | solution.py:63
  40.7 1.0 fusion.64
  41.6 1.0 fusion.62
  42.7 18.1 %all-to-all-done = bf16[32,1,2,8,768]{4,2,3,1,0:T(2,128)(2,1)S(1)} async-done(((bf16[32,1,2,8,768]{4,2,3,1,0:T(2,128)(2,1)}), bf16[32,1,2,8,768]{4,2,3,1,0:T(2,128)(2,1)S(1)}, u32[]{:S(2)}, u32[]{:S(2)}) %all-to-all-start) | async-done | bytes 786464 | tf_op jit(solution)/shard_map/all_to_all | solution.py:63
  61.1 16.0 %while.10 = (s32[]{:T(128)}, f32[704,512]{1,0:T(8,128)S(1)}, s32[]{:T(128)}, bf16[704,768]{1,0:T(8,128)(2,1)}, bf16[512,768]{1,0:T(8,128)(2,1)S(1)}, /*index=5*/...) while((s32[]{:T(128)}, f32[704,512]{1,0:T(8,128)S(1)}, s32[]{:T(128)}, ...), condition=%wide.region_1.2_spmd, body=%wide.region_0.1_spmd.sunk | while | flops 83951752 | bytes 1541851 | solution.py:86
  61.2 1.4 %convolution_dynamic-update-slice_fusion.2 = f32[704,512]{1,0:T(8,128)S(1)} fusion(f32[704,512]{1,0:T(8,128)S(1)} %get-tuple-element.140, s32[]{:T(128)S(6)} %select_n.82, bf16[512,512]{1,0:T(8,128)(2,1)S(1)} %get-tuple-element.154, bf16[512,768]{1,0:T(8,128)(2,1)S(1)} %get-tuple-element.153, bf16[704,768]{1,0:T(8,128)(2,1)} %get-tuple-element.152, ...), kind=kOutput, calls=%fused_computation.clone.1 | convolution fusion | flops 83951616 | bytes 1541632 | tf_op jit(solution)/shard_map/while/body/dot_general | solution.py:81
  62.6 1.4 %convolution_dynamic-update-slice_fusion.2 = f32[704,512]{1,0:T(8,128)S(1)} fusion(f32[704,512]{1,0:T(8,128)S(1)} %get-tuple-element.140, s32[]{:T(128)S(6)} %select_n.82, bf16[512,512]{1,0:T(8,128)(2,1)S(1)} %get-tuple-element.154, bf16[512,768]{1,0:T(8,128)(2,1)S(1)} %get-tuple-element.153, bf16[704,768]{1,0:T(8,128)(2,1)} %get-tuple-element.152, ...), kind=kOutput, calls=%fused_computation.clone.1 | convolution fusion | flops 83951616 | bytes 1541632 | tf_op jit(solution)/shard_map/while/body/dot_general | solution.py:81
  64.1 1.4 %convolution_dynamic-update-slice_fusion.2 = f32[704,512]{1,0:T(8,128)S(1)} fusion(f32[704,512]{1,0:T(8,128)S(1)} %get-tuple-element.140, s32[]{:T(128)S(6)} %select_n.82, bf16[512,512]{1,0:T(8,128)(2,1)S(1)} %get-tuple-element.154, bf16[512,768]{1,0:T(8,128)(2,1)S(1)} %get-tuple-element.153, bf16[704,768]{1,0:T(8,128)(2,1)} %get-tuple-element.152, ...), kind=kOutput, calls=%fused_computation.clone.1 | convolution fusion | flops 83951616 | bytes 1541632 | tf_op jit(solution)/shard_map/while/body/dot_general | solution.py:81
  65.5 1.4 %convolution_dynamic-update-slice_fusion.2 = f32[704,512]{1,0:T(8,128)S(1)} fusion(f32[704,512]{1,0:T(8,128)S(1)} %get-tuple-element.140, s32[]{:T(128)S(6)} %select_n.82, bf16[512,512]{1,0:T(8,128)(2,1)S(1)} %get-tuple-element.154, bf16[512,768]{1,0:T(8,128)(2,1)S(1)} %get-tuple-element.153, bf16[704,768]{1,0:T(8,128)(2,1)} %get-tuple-element.152, ...), kind=kOutput, calls=%fused_computation.clone.1 | convolution fusion | flops 83951616 | bytes 1541632 | tf_op jit(solution)/shard_map/while/body/dot_general | solution.py:81
  67.0 1.4 %convolution_dynamic-update-slice_fusion.2 = f32[704,512]{1,0:T(8,128)S(1)} fusion(f32[704,512]{1,0:T(8,128)S(1)} %get-tuple-element.140, s32[]{:T(128)S(6)} %select_n.82, bf16[512,512]{1,0:T(8,128)(2,1)S(1)} %get-tuple-element.154, bf16[512,768]{1,0:T(8,128)(2,1)S(1)} %get-tuple-element.153, bf16[704,768]{1,0:T(8,128)(2,1)} %get-tuple-element.152, ...), kind=kOutput, calls=%fused_computation.clone.1 | convolution fusion | flops 83951616 | bytes 1541632 | tf_op jit(solution)/shard_map/while/body/dot_general | solution.py:81
  68.4 1.4 %convolution_dynamic-update-slice_fusion.2 = f32[704,512]{1,0:T(8,128)S(1)} fusion(f32[704,512]{1,0:T(8,128)S(1)} %get-tuple-element.140, s32[]{:T(128)S(6)} %select_n.82, bf16[512,512]{1,0:T(8,128)(2,1)S(1)} %get-tuple-element.154, bf16[512,768]{1,0:T(8,128)(2,1)S(1)} %get-tuple-element.153, bf16[704,768]{1,0:T(8,128)(2,1)} %get-tuple-element.152, ...), kind=kOutput, calls=%fused_computation.clone.1 | convolution fusion | flops 83951616 | bytes 1541632 | tf_op jit(solution)/shard_map/while/body/dot_general | solution.py:81
  69.9 1.4 %convolution_dynamic-update-slice_fusion.2 = f32[704,512]{1,0:T(8,128)S(1)} fusion(f32[704,512]{1,0:T(8,128)S(1)} %get-tuple-element.140, s32[]{:T(128)S(6)} %select_n.82, bf16[512,512]{1,0:T(8,128)(2,1)S(1)} %get-tuple-element.154, bf16[512,768]{1,0:T(8,128)(2,1)S(1)} %get-tuple-element.153, bf16[704,768]{1,0:T(8,128)(2,1)} %get-tuple-element.152, ...), kind=kOutput, calls=%fused_computation.clone.1 | convolution fusion | flops 83951616 | bytes 1541632 | tf_op jit(solution)/shard_map/while/body/dot_general | solution.py:81
  71.3 1.4 %convolution_dynamic-update-slice_fusion.2 = f32[704,512]{1,0:T(8,128)S(1)} fusion(f32[704,512]{1,0:T(8,128)S(1)} %get-tuple-element.140, s32[]{:T(128)S(6)} %select_n.82, bf16[512,512]{1,0:T(8,128)(2,1)S(1)} %get-tuple-element.154, bf16[512,768]{1,0:T(8,128)(2,1)S(1)} %get-tuple-element.153, bf16[704,768]{1,0:T(8,128)(2,1)} %get-tuple-element.152, ...), kind=kOutput, calls=%fused_computation.clone.1 | convolution fusion | flops 83951616 | bytes 1541632 | tf_op jit(solution)/shard_map/while/body/dot_general | solution.py:81
  72.8 1.4 %convolution_dynamic-update-slice_fusion.2 = f32[704,512]{1,0:T(8,128)S(1)} fusion(f32[704,512]{1,0:T(8,128)S(1)} %get-tuple-element.140, s32[]{:T(128)S(6)} %select_n.82, bf16[512,512]{1,0:T(8,128)(2,1)S(1)} %get-tuple-element.154, bf16[512,768]{1,0:T(8,128)(2,1)S(1)} %get-tuple-element.153, bf16[704,768]{1,0:T(8,128)(2,1)} %get-tuple-element.152, ...), kind=kOutput, calls=%fused_computation.clone.1 | convolution fusion | flops 83951616 | bytes 1541632 | tf_op jit(solution)/shard_map/while/body/dot_general | solution.py:81
  74.2 1.4 %convolution_dynamic-update-slice_fusion.2 = f32[704,512]{1,0:T(8,128)S(1)} fusion(f32[704,512]{1,0:T(8,128)S(1)} %get-tuple-element.140, s32[]{:T(128)S(6)} %select_n.82, bf16[512,512]{1,0:T(8,128)(2,1)S(1)} %get-tuple-element.154, bf16[512,768]{1,0:T(8,128)(2,1)S(1)} %get-tuple-element.153, bf16[704,768]{1,0:T(8,128)(2,1)} %get-tuple-element.152, ...), kind=kOutput, calls=%fused_computation.clone.1 | convolution fusion | flops 83951616 | bytes 1541632 | tf_op jit(solution)/shard_map/while/body/dot_general | solution.py:81
  75.7 1.4 %convolution_dynamic-update-slice_fusion.2 = f32[704,512]{1,0:T(8,128)S(1)} fusion(f32[704,512]{1,0:T(8,128)S(1)} %get-tuple-element.140, s32[]{:T(128)S(6)} %select_n.82, bf16[512,512]{1,0:T(8,128)(2,1)S(1)} %get-tuple-element.154, bf16[512,768]{1,0:T(8,128)(2,1)S(1)} %get-tuple-element.153, bf16[704,768]{1,0:T(8,128)(2,1)} %get-tuple-element.152, ...), kind=kOutput, calls=%fused_computation.clone.1 | convolution fusion | flops 83951616 | bytes 1541632 | tf_op jit(solution)/shard_map/while/body/dot_general | solution.py:81
  77.1 2.5 %collective-permute-start.1 = (f32[1,704,512]{2,1,0:T(8,128)S(1)}, f32[1,704,512]{2,1,0:T(8,128)S(1)}, u32[]{:S(2)}, u32[]{:S(2)}) collective-permute-start(f32[1,704,512]{2,1,0:T(8,128)S(1)} %bitcast.146), channel_id=1, source_target_pairs={{1,0},{2,1},{3,2},{4,3},{5,4},{6,5},{7,6},{8,7},{9,8},{10,9},{11,1... | collective-permute-start | bytes 4325384 | tf_op jit(solution)/shard_map/ppermute | solution.py:21
  79.7 3.0 %collective-permute-start = (f32[1,704,512]{2,1,0:T(8,128)S(1)}, f32[1,704,512]{2,1,0:T(8,128)S(1)}, u32[]{:S(2)}, u32[]{:S(2)}) collective-permute-start(f32[1,704,512]{2,1,0:T(8,128)S(1)} %bitcast.147), channel_id=1, source_target_pairs={{0,1},{1,2},{2,3},{3,4},{4,5},{5,6},{6,7},{7,8},{8,9},{9,10},{10,1... | collective-permute-start | bytes 4325384 | tf_op jit(solution)/shard_map/ppermute | solution.py:19
  83.1 25.7 %collective-permute-done.1 = f32[1,704,512]{2,1,0:T(8,128)S(1)} collective-permute-done((f32[1,704,512]{2,1,0:T(8,128)S(1)}, f32[1,704,512]{2,1,0:T(8,128)S(1)}, u32[]{:S(2)}, u32[]{:S(2)}) %collective-permute-start.1) | collective-permute-done | bytes 1441824 | tf_op jit(solution)/shard_map/ppermute | solution.py:21
  108.8 4.8 %collective-permute-done = f32[1,704,512]{2,1,0:T(8,128)S(1)} collective-permute-done((f32[1,704,512]{2,1,0:T(8,128)S(1)}, f32[1,704,512]{2,1,0:T(8,128)S(1)}, u32[]{:S(2)}, u32[]{:S(2)}) %collective-permute-start) | collective-permute-done | bytes 1441824 | tf_op jit(solution)/shard_map/ppermute | solution.py:19
  114.2 8.4 %fusion.10 = f32[1,704,512]{2,1,0:T(8,128)} fusion(f32[3,716,512]{2,1,0:T(8,128)S(1)} %select_maximum_fusion, f32[1,704,512]{2,1,0:T(8,128)S(1)} %collective-permute-done.1, f32[704,512]{1,0:T(8,128)S(1)} %get-tuple-element.37, f32[1,704,512]{2,1,0:T(8,128)S(1)} %collective-permute-done, f32[704]{0:T(1024)S(1)} %get-tuple-element.39, ...), kind=kLoop, calls=%fused_computation.16 | loop fusion | flops 28114944 | bytes 57782208 | tf_op jit(solution)/shard_map/jit(_where)/select_n | solution.py:102
  (48 shorter events, 16.2 us)
Async XLA Ops:
  33.6 27.3 %all-to-all-start = ((bf16[32,1,2,8,768]{4,2,3,1,0:T(2,128)(2,1)}), bf16[32,1,2,8,768]{4,2,3,1,0:T(2,128)(2,1)S(1)}, u32[]{:S(2)}, u32[]{:S(2)}) async-start(bf16[32,1,2,8,768]{4,2,3,1,0:T(2,128)(2,1)} %constant_dynamic-update-slice_fusion), calls=%async_computation | async-start | bytes 1572864 | tf_op jit(solution)/shard_map/all_to_all | solution.py:63
  61.1 21.6 %copy-start = (f32[1,3,13,704]{3,0,2,1:T(1,128)S(1)}, f32[1,3,13,704]{3,0,2,1:T(1,128)}, u32[]{:S(2)}) copy-start(f32[1,3,13,704]{3,0,2,1:T(1,128)} %param.7) | copy-start | bytes 329476
  77.1 31.7 %collective-permute-start.1 = (f32[1,704,512]{2,1,0:T(8,128)S(1)}, f32[1,704,512]{2,1,0:T(8,128)S(1)}, u32[]{:S(2)}, u32[]{:S(2)}) collective-permute-start(f32[1,704,512]{2,1,0:T(8,128)S(1)} %bitcast.146), channel_id=1, source_target_pairs={{1,0},{2,1},{3,2},{4,3},{5,4},{6,5},{7,6},{8,7},{9,8},{10,9},{11,1... | collective-permute-start | bytes 4325384 | tf_op jit(solution)/shard_map/ppermute | solution.py:21
  79.7 34.0 %collective-permute-start = (f32[1,704,512]{2,1,0:T(8,128)S(1)}, f32[1,704,512]{2,1,0:T(8,128)S(1)}, u32[]{:S(2)}, u32[]{:S(2)}) collective-permute-start(f32[1,704,512]{2,1,0:T(8,128)S(1)} %bitcast.147), channel_id=1, source_target_pairs={{0,1},{1,2},{2,3},{3,4},{4,5},{5,6},{6,7},{7,8},{8,9},{9,10},{10,1... | collective-permute-start | bytes 4325384 | tf_op jit(solution)/shard_map/ppermute | solution.py:19
